TPU v7x, 512 devices: a whole 4x4x16 slice. The times are simulated.
512 devices in a mesh: req: 32 (over z, core), mlp: 16 (over y, x).
Axes of the slice: x: 4, y: 4, z: 16, core: 2. Of those that a mesh axis runs over, the one named last changes fastest.
Arguments:
- hidden_input: bfloat16 [12288, 4096], P('req', 'mlp'), may hold values from -6 to 6
- input_norm_gain: bfloat16 [4096], replicated, may hold values from 0.099609375 to 1.8984375
- query_norm_gain: bfloat16 [128], replicated, may hold values from 0.099609375 to 1.8984375
- key_norm_gain: bfloat16 [128], replicated, may hold values from 0.099609375 to 1.8984375
- query_weight: bfloat16 [4096, 4096], P('req', 'mlp'), may hold values from -0.09375 to 0.09375
- key_value_weight: bfloat16 [4096, 2, 1024], P('req'), may hold values from -0.09375 to 0.09375
- output_weight: bfloat16 [4096, 16, 256], P('mlp', None, 'req'), may hold values from -0.09375 to 0.09375
- adapter_down_qkv: bfloat16 [64, 48, 4096], P('req', None, 'mlp'), may hold values from -0.09375 to 0.09375
- adapter_down_output: bfloat16 [64, 16, 4096], P('req', None, 'mlp'), may hold values from -0.09375 to 0.09375
- adapter_up_query: bfloat16 [64, 16, 4096], P('req', None, 'mlp'), may hold values from -1.5 to 1.5
- adapter_up_key_value: bfloat16 [64, 16, 2, 1024], P('req'), may hold values from -1.5 to 1.5
- adapter_up_output: bfloat16 [64, 16, 4096], P('req', None, 'mlp'), may hold values from -1.5 to 1.5
- pool: bfloat16 [16384, 2, 1024], P('req'), may hold values from -6 to 6
- lengths: int32 [32, 4], P('req'), may hold values from 1 to 192, 384 in all within a row
- cached_prefix_pages: int32 [32, 4], P('req'), may hold values from 0 to 8
- prefix_page_table: int32 [32, 4, 8], P('req'), may hold values from 0 to 7, each once within a row
- adapter_of_request: int32 [32, 4, 1], P('req'), may hold values from 0 to 63
- adapter_storage: int32 [64], replicated, may hold values from 0 to 63, each once
Outputs:
- attention_update: bfloat16 [12288, 4096], P('req', 'mlp')
- new_cache: bfloat16 [12288, 2, 1024], P('req', None, 'mlp')
Inputs may be any that keep to these rules, and one draw needn't show every extreme that they name: The lengths of one index of req sum to 384, and the longest of them is 192. `prefix_page_table`: each row lists every page of its pool once. `adapter_of_request`: every adapter is used by some request. `adapter_storage`: each slot holds one adapter.
All inputs are finite; a program needn't handle non-finite values.
Results may differ from a plain program's by a relative error of at most 0.035.
Values may be sent and summed in bfloat16 or wider, within the bound.
A program may use at most 64 MiB of HBM per device.

v0:
```python
import math
import jax
import jax.numpy as jnp
from jax import lax
from jax.sharding import PartitionSpec as P

QUERY_HEADS = 32
KEY_VALUE_HEADS = 8
HEAD_SIZE = 128
ADAPTER_RANK = 16
PAGE = 64
epsilon = 1e-06
rope_base = 1000000.0


def root_mean_scale(values, gain_vec):
    mean_sq = jnp.mean(values * values, axis=-1, keepdims=True)
    return values * lax.rsqrt(mean_sq + epsilon) * gain_vec.astype(jnp.float32)


def rotary_embed(values, token_positions):
    half_width = values.shape[-1] // 2
    inverse_freq = jnp.exp(
        jnp.arange(half_width, dtype=jnp.float32) * (-2.0 / values.shape[-1]) * math.log(rope_base)
    )
    angles = token_positions.astype(jnp.float32)[:, None] * inverse_freq[None, :]
    cosine = jnp.cos(angles)[:, None, :]
    sine_part = jnp.sin(angles)[:, None, :]
    front = values[..., :half_width]
    back = values[..., half_width:]
    return jnp.concatenate(
        [front * cosine - back * sine_part, back * cosine + front * sine_part], axis=-1
    )


def row_tables(lengths_row, prefix_row, page_rows, row_count):
    ends_at = jnp.cumsum(lengths_row)
    starts_at = ends_at - lengths_row
    row_ids = jnp.arange(row_count, dtype=jnp.int32)
    owners = jnp.sum((row_ids[:, None] >= ends_at[None, :]).astype(jnp.int32), axis=1)
    group_members = owners[:, None] == jnp.arange(lengths_row.shape[0], dtype=jnp.int32)[None, :]
    offsets = PAGE * prefix_row[None, :] + row_ids[:, None] - starts_at[None, :]
    token_positions = jnp.sum(jnp.where(group_members, offsets, 0), axis=1)
    page_ids = jnp.arange(page_rows.shape[1], dtype=jnp.int32)
    listed = (page_rows[:, :, None] == page_ids[None, None, :]) & (
        page_ids[None, :, None] < prefix_row[:, None, None]
    )
    page_used = jnp.sum(listed.astype(jnp.float32), axis=1)
    return (owners, group_members, token_positions, page_used)


def apply_adapter(lowrank_inner, group_members, chosen_up):
    masked = lowrank_inner[:, None, :] * group_members.astype(lowrank_inner.dtype)[:, :, None]
    return jnp.einsum("gjr,jrc->gc", masked, chosen_up, preferred_element_type=jnp.float32)


def select_rows(terms, group_members):
    return jnp.sum(terms * group_members.astype(jnp.float32)[:, :, None], axis=1)


def shards(
    hidden_input,
    input_norm_gain,
    query_norm_gain,
    key_norm_gain,
    query_weight,
    key_value_weight,
    output_weight,
    adapter_down_qkv,
    adapter_down_output,
    adapter_up_query,
    adapter_up_key_value,
    adapter_up_output,
    pool,
    lengths,
    cached_prefix_pages,
    prefix_page_table,
    adapter_of_request,
    adapter_storage,
):
    feature_group_count = lax.axis_size("mlp")
    feature_group_index = lax.axis_index("mlp")
    whole = lax.all_gather(hidden_input, "mlp", axis=1, tiled=True)
    row_count, full_width = whole.shape
    normalized_input = root_mean_scale(whole.astype(jnp.float32), input_norm_gain).astype(
        jnp.bfloat16
    )
    owners, group_members, token_positions, page_used = row_tables(
        lengths[0], cached_prefix_pages[0], prefix_page_table[0], row_count
    )
    q_width = query_weight.shape[1]
    query_head_rows = q_width // HEAD_SIZE
    key_value_local = max(1, KEY_VALUE_HEADS // feature_group_count)
    key_value_width = key_value_local * HEAD_SIZE
    key_value_begin = (
        feature_group_index * query_head_rows // (QUERY_HEADS // KEY_VALUE_HEADS) * HEAD_SIZE
    )
    own_wkv = lax.dynamic_slice_in_dim(key_value_weight, key_value_begin, key_value_width, 2)
    request_key_value_up = lax.dynamic_slice_in_dim(
        adapter_up_key_value, key_value_begin, key_value_width, 3
    )
    gathered = (
        lax.all_gather(adapter_down_qkv, "req", axis=0, tiled=True),
        lax.all_gather(adapter_down_output, "req", axis=0, tiled=True),
        lax.all_gather(adapter_up_query, "req", axis=0, tiled=True),
        lax.all_gather(request_key_value_up, "req", axis=0, tiled=True),
        lax.all_gather(adapter_up_output, "req", axis=0, tiled=True),
    )
    slot_indices = jnp.take(adapter_storage, adapter_of_request[0, :, 0], axis=0)
    chosen_down = jnp.take(gathered[0], slot_indices, axis=0)
    output_down = jnp.take(gathered[1], slot_indices, axis=0)
    query_up_part = jnp.take(gathered[2], slot_indices, axis=0)
    key_value_up = jnp.take(gathered[3], slot_indices, axis=0)
    output_up = jnp.take(gathered[4], slot_indices, axis=0)
    feature_cols = full_width // feature_group_count
    own_normed = lax.dynamic_slice_in_dim(
        normalized_input, feature_group_index * feature_cols, feature_cols, 1
    )
    low_terms = jnp.einsum(
        "gd,jkd->gjk", own_normed, chosen_down, preferred_element_type=jnp.float32
    )
    lowrank_inner = lax.psum(select_rows(low_terms, group_members).astype(jnp.bfloat16), "mlp")
    q_part = lax.all_gather(query_weight, "req", axis=0, tiled=True)
    kv_part = lax.all_gather(own_wkv, "req", axis=0, tiled=True)
    query_width_total = jnp.dot(normalized_input, q_part, preferred_element_type=jnp.float32)
    kv_total = jnp.dot(
        normalized_input,
        kv_part.reshape(kv_part.shape[0], 2 * key_value_width),
        preferred_element_type=jnp.float32,
    )
    query_width_total, kv_total = (query_width_total, kv_total)
    query_plain = (
        query_width_total
        + apply_adapter(lowrank_inner[:, 0:ADAPTER_RANK], group_members, query_up_part)
    ).astype(jnp.bfloat16)
    key_lowrank_part = apply_adapter(
        lowrank_inner[:, ADAPTER_RANK : 2 * ADAPTER_RANK], group_members, key_value_up[:, :, 0]
    )
    value_lowrank_part = apply_adapter(
        lowrank_inner[:, 2 * ADAPTER_RANK : 3 * ADAPTER_RANK], group_members, key_value_up[:, :, 1]
    )
    key_value_plain = (
        kv_total.reshape(row_count, 2, key_value_width)
        + jnp.stack([key_lowrank_part, value_lowrank_part], axis=1)
    ).astype(jnp.bfloat16)
    cached = lax.dynamic_slice_in_dim(pool, key_value_begin, key_value_width, 2)
    pool_token_rows = cached.shape[0]
    query_rotated = rotary_embed(
        root_mean_scale(
            query_plain.astype(jnp.float32).reshape(row_count, query_head_rows, HEAD_SIZE),
            query_norm_gain,
        ),
        token_positions,
    ).astype(jnp.bfloat16)
    key_rotated = rotary_embed(
        root_mean_scale(
            key_value_plain[:, 0]
            .astype(jnp.float32)
            .reshape(row_count, key_value_local, HEAD_SIZE),
            key_norm_gain,
        ),
        token_positions,
    ).astype(jnp.bfloat16)
    cache_columns = KEY_VALUE_HEADS * HEAD_SIZE // feature_group_count
    own_offset = feature_group_index * cache_columns - key_value_begin
    local_cache = jnp.stack(
        [key_rotated.reshape(row_count, key_value_width), key_value_plain[:, 1]], axis=1
    )
    new_cache = lax.dynamic_slice_in_dim(local_cache, own_offset, cache_columns, 2)
    key_matrix = jnp.concatenate(
        [cached[:, 0].reshape(pool_token_rows, key_value_local, HEAD_SIZE), key_rotated], axis=0
    )
    value_matrix = jnp.concatenate(
        [
            cached[:, 1].reshape(pool_token_rows, key_value_local, HEAD_SIZE),
            key_value_plain[:, 1].reshape(row_count, key_value_local, HEAD_SIZE),
        ],
        axis=0,
    )
    pool_ok = jnp.dot(group_members.astype(jnp.float32), page_used, precision=lax.Precision.HIGHEST)
    pool_ok = jnp.repeat(pool_ok, PAGE, axis=1) > 0.5
    row_ids = jnp.arange(row_count, dtype=jnp.int32)
    causal = (owners[:, None] == owners[None, :]) & (row_ids[None, :] <= row_ids[:, None])
    allowed = jnp.concatenate([pool_ok, causal], axis=1)
    query_rows = query_rotated.reshape(
        row_count, key_value_local, query_head_rows // key_value_local, HEAD_SIZE
    )
    scores = jnp.einsum(
        "gkhd,skd->khgs", query_rows, key_matrix, preferred_element_type=jnp.float32
    ) / math.sqrt(HEAD_SIZE)
    exp_scores = jnp.where(allowed[None, None], jnp.exp(scores), 0.0)
    softmax = (exp_scores / jnp.sum(exp_scores, axis=-1, keepdims=True)).astype(jnp.bfloat16)
    attended = jnp.einsum(
        "khgs,skd->gkhd", softmax, value_matrix, preferred_element_type=jnp.float32
    )
    attended = attended.astype(jnp.bfloat16).reshape(row_count, q_width)
    out_terms = jnp.einsum("gc,jrc->gjr", attended, output_down, preferred_element_type=jnp.float32)
    lowrank_result = lax.psum(select_rows(out_terms, group_members), "mlp").astype(jnp.bfloat16)
    partial_value = jnp.einsum(
        "gc,cnk->gnk",
        attended,
        lax.all_gather(output_weight, "req", axis=2, tiled=True),
        preferred_element_type=jnp.float32,
    )
    summed_output = lax.psum_scatter(
        partial_value.reshape(row_count, full_width).astype(jnp.bfloat16),
        "mlp",
        scatter_dimension=1,
        tiled=True,
    ).astype(jnp.float32)
    attention_update = (
        summed_output + apply_adapter(lowrank_result, group_members, output_up)
    ).astype(jnp.bfloat16)
    return (attention_update, new_cache)


def solution(mesh):
    return jax.shard_map(
        shards,
        mesh=mesh,
        in_specs=(
            P("req", "mlp"),
            P(),
            P(),
            P(),
            P("req", "mlp"),
            P("req", None, None),
            P("mlp", None, "req"),
            P("req", None, "mlp"),
            P("req", None, "mlp"),
            P("req", None, "mlp"),
            P("req", None, None, None),
            P("req", None, "mlp"),
            P("req", None, None),
            P("req", None),
            P("req", None),
            P("req", None, None),
            P("req", None, None),
            P(),
        ),
        out_specs=(P("req", "mlp"), P("req", None, "mlp")),
        check_vma=False,
    )
```

profile of v0, /device:TPU:32, one launch (start us, length us, event | category | flops | bytes accessed | tf_op | source)
XLA Modules:
  0.0 518.9 jit_solution(2938642543624137017)
XLA Ops:
  11.6 1.3 gather_fusion
  14.2 0.8 reduce-window.4
  16.5 0.7 constant_dynamic-slice_fusion.1
  17.3 36.1 %all_gather.30 = bf16[64,16,2,128]{3,1,2,0:T(8,128)(2,1)S(1)} all-gather(bf16[2,16,2,128]{3,1,2,0:T(8,128)(2,1)S(1)} %copy.66), channel_id=1, replica_groups=mesh['req'=32,'mlp'=16] {'req'}, dimensions={0}, use_global_device_ids=true | all-gather | bytes 540672 | tf_op jit(solution)/shard_map/all_gather | solution.py:106
  53.3 0.7 convert_element_type.100
  54.0 1.2 convert_element_type.109
  56.0 1.6 constant_dynamic-slice_fusion
  57.6 30.2 %all_gather.32 = bf16[64,16,256]{2,1,0:T(8,128)(2,1)S(1)} all-gather(bf16[2,16,256]{2,1,0:T(8,128)(2,1)S(1)} %copy-done.6), channel_id=1, replica_groups=mesh['req'=32,'mlp'=16] {'req'}, dimensions={0}, use_global_device_ids=true | all-gather | bytes 540672 | tf_op jit(solution)/shard_map/all_gather | solution.py:105
  90.7 1.2 gather_fusion.3
  91.8 0.8 multiply_cosine_fusion
  92.8 2.6 gather_fusion.1
  95.4 61.2 %all-gather.8.cloned.1.call-done = bf16[4096,2,128]{2,1,0:T(2,128)(2,1)} async-done(((bf16[128,2,128]{2,1,0:T(2,128)(2,1)}), bf16[4096,2,128]{2,1,0:T(2,128)(2,1)}) %all-gather.8.cloned.1.call-update) | async-done | bytes 2097168 | tf_op jit(solution)/shard_map/all_gather | solution.py:124
  156.6 4.7 copy.61
  161.3 63.1 %all-gather.6.cloned.1.call-done = bf16[384,4096]{1,0:T(8,128)(2,1)} async-done(((bf16[384,256]{1,0:T(8,128)(2,1)}), bf16[384,4096]{1,0:T(8,128)(2,1)}) %all-gather.6.cloned.1.call-update) | async-done | bytes 3145744 | tf_op jit(solution)/shard_map/all_gather | solution.py:83
  224.4 2.7 fusion
  227.3 1.1 fusion.2
  228.4 1.6 copy-done.2
  230.0 0.9 fusion.26
  230.9 72.8 %psum.14 = bf16[384,48]{0,1:T(8,128)(2,1)S(1)} all-reduce(bf16[384,48]{0,1:T(8,128)(2,1)} %fusion.26), channel_id=1, replica_groups=mesh['req'=32,'mlp'=16] {'mlp'}, use_global_device_ids=true, to_apply=%region_4.5 | all-reduce | flops 18432 | bytes 73728 | tf_op jit(solution)/shard_map/psum | solution.py:122
  303.7 0.9 convolution_bitcast_fusion.2
  304.7 0.9 convolution_bitcast_fusion.3
  305.6 3.2 fusion.17
  309.6 3.8 fusion.92
  314.5 0.9 fusion.5
  315.5 0.9 fusion.23
  316.4 53.5 %all-gather.14.cloned.1.call-done = bf16[256,16,256]{0,2,1:T(8,128)(2,1)} async-done(((bf16[256,16,8]{0,2,1:T(8,128)(2,1)}), bf16[256,16,256]{0,2,1:T(8,128)(2,1)}) %all-gather.14.cloned.1.call-update) | async-done | bytes 2097168 | tf_op jit(solution)/shard_map/all_gather | solution.py:202
  369.9 4.3 convolution_convert_fusion
  374.9 28.9 %all_gather.34 = bf16[64,16,256]{2,1,0:T(8,128)(2,1)S(1)} all-gather(bf16[2,16,256]{2,1,0:T(8,128)(2,1)S(1)} %copy-done.7), channel_id=1, replica_groups=mesh['req'=32,'mlp'=16] {'req'}, dimensions={0}, use_global_device_ids=true | all-gather | bytes 540672 | tf_op jit(solution)/shard_map/all_gather | solution.py:104
  404.3 30.1 %all_gather.35 = bf16[64,16,256]{2,1,0:T(8,128)(2,1)S(1)} all-gather(bf16[2,16,256]{2,1,0:T(8,128)(2,1)S(1)} %copy-done.8), channel_id=1, replica_groups=mesh['req'=32,'mlp'=16] {'req'}, dimensions={0}, use_global_device_ids=true | all-gather | bytes 540672 | tf_op jit(solution)/shard_map/all_gather | solution.py:107
  435.2 74.3 %psum.15 = bf16[384,16]{0,1:T(8,128)(2,1)S(1)} all-reduce(f32[384,16]{0,1:T(8,128)S(1)} %fusion.27), channel_id=1, replica_groups=mesh['req'=32,'mlp'=16] {'mlp'}, use_global_device_ids=true, to_apply=%region_12.14 | all-reduce | flops 6144 | bytes 36864 | tf_op jit(solution)/shard_map/psum | solution.py:198
  509.5 0.7 fusion.50
  510.2 1.9 fusion.16
  (94 shorter events, 14.7 us)
Async XLA Ops:
  7.2 1.1 copy-start
  7.2 81.2 %copy-start.17 = (s32[1,4]{1,0:T(1,128)S(1)}, s32[1,4]{1,0:T(1,128)}, u32[]{:S(2)}) copy-start(s32[1,4]{1,0:T(1,128)} %param.34) | copy-start | bytes 52
  7.2 50.4 %copy-start.6 = (bf16[2,16,256]{2,1,0:T(8,128)(2,1)S(1)}, bf16[2,16,256]{2,1,0:T(8,128)(2,1)}, u32[]{:S(2)}) copy-start(bf16[2,16,256]{2,1,0:T(8,128)(2,1)} %param.29) | copy-start | bytes 49156
  7.2 80.6 %copy-start.16 = (bf16[128]{0:T(256)(128)(2,1)S(1)}, bf16[128]{0:T(256)(128)(2,1)}, u32[]{:S(2)}) copy-start(bf16[128]{0:T(256)(128)(2,1)} %param.22) | copy-start | bytes 772
  7.2 81.2 %copy-start.13 = (s32[1,4,8]{2,1,0:T(4,128)S(1)}, s32[1,4,8]{2,1,0:T(4,128)}, u32[]{:S(2)}) copy-start(s32[1,4,8]{2,1,0:T(4,128)} %param.35) | copy-start | bytes 388
  7.2 85.5 %all-gather.10.cloned.1.call-start = ((), (), s32[]{:S(2)}) async-start(), calls=%async_computation.3 | async-start | bytes 1622016 | tf_op jit(solution)/shard_map/all_gather | solution.py:103
  8.0 148.6 %all-gather.8.cloned.1.call-start = ((), (), s32[]{:S(2)}) async-start(), calls=%async_computation.2 | async-start | bytes 2162688 | tf_op jit(solution)/shard_map/all_gather | solution.py:124
  8.9 215.5 %all-gather.6.cloned.1.call-start = ((), (), s32[]{:S(2)}) async-start(), calls=%async_computation.1 | async-start | bytes 3342336 | tf_op jit(solution)/shard_map/all_gather | solution.py:83
  9.7 299.9 %all-gather.12.cloned.1.call-start = ((), (), s32[]{:S(2)}) async-start(), calls=%async_computation.4 | async-start | bytes 2162688 | tf_op jit(solution)/shard_map/all_gather | solution.py:123
  10.3 359.6 %all-gather.14.cloned.1.call-start = ((), (), s32[]{:S(2)}) async-start(), calls=%async_computation.5 | async-start | bytes 2162688 | tf_op jit(solution)/shard_map/all_gather | solution.py:202
  10.8 499.4 %reduce-scatter.2.cloned.1.call-start = ((), (), s32[]{:S(2)}) async-start(), calls=%async_computation.6 | async-start | bytes 3342336 | tf_op jit(solution)/shard_map/reduce_scatter | solution.py:205
  14.2 147.1 %copy-start.11 = (f32[64]{0:T(128)}, f32[64]{0:T(128)S(1)}, u32[]{:S(2)}) copy-start(f32[64]{0:T(128)S(1)} %multiply_exponential_fusion) | copy-start | bytes 772
  224.4 2.8 copy-start.1
  227.3 2.8 copy-start.5
  227.3 2.8 copy-start.9
  228.4 1.7 copy-start.2
  305.6 3.3 copy-start.14
  305.6 3.4 copy-start.12
  309.6 3.9 copy-start.4
  309.6 4.5 copy-start.15
  314.3 1.2 copy-start.3
  374.1 0.7 copy-start.7
  374.1 30.2 %copy-start.8 = (bf16[2,16,256]{2,1,0:T(8,128)(2,1)S(1)}, bf16[2,16,256]{2,1,0:T(8,128)(2,1)}, u32[]{:S(2)}) copy-start(bf16[2,16,256]{2,1,0:T(8,128)(2,1)} %param.31) | copy-start | bytes 49156
  374.1 60.9 %copy-start.10 = (f32[384,4]{0,1:T(4,128)S(1)}, f32[384,4]{0,1:T(4,128)}, u32[]{:S(2)}) copy-start(f32[384,4]{0,1:T(4,128)} %get-tuple-element.17) | copy-start | bytes 18436
Sparse Core Ops, SparseCore 0:
  10.2 75.3 all-gather.9
  87.7 68.8 all-gather.7
  159.6 64.8 all-gather.5
  226.4 71.1 all-gather.11
  299.5 70.3 all-gather.13
  374.3 87.2 reduce-scatter.1
where the time goes:
time: 520 us; the launch traced here: 519 us
  blocking collectives  272 us (52%)
  waiting for transfers between devices  180 us (35%)
  matrix products  18.5 us (4%)
  local copies, waits for them, and re-layouts  18.3 us (4%)
  other arithmetic  14.7 us (3%)
  between operations  14.6 us (3%)
    psum x1, blocking collectives, shards(): lax.psum(select_rows(out_terms, group_members), 'mlp').astype(jnp.bfloat16)  74.3 us
    psum x1, blocking collectives, shards(): lax.psum(select_rows(low_terms, group_members).astype(jnp.bfloat16), 'mlp')  72.8 us
    all_gather x1, waiting for transfers between devices, shards(): whole = lax.all_gather(hidden_input, 'mlp', axis=1, tiled=True)  63.1 us
    all_gather x1, waiting for transfers between devices, shards(): kv_part = lax.all_gather(own_wkv, 'req', axis=0, tiled=True)  61.2 us
    all_gather x1, waiting for transfers between devices, shards(): lax.all_gather(output_weight, 'req', axis=2, tiled=True)  53.5 us
    all_gather x1, blocking collectives, shards(): lax.all_gather(request_key_value_up, 'req', axis=0, tiled=True)  36.1 us
    all_gather x1, blocking collectives, shards(): lax.all_gather(adapter_up_query, 'req', axis=0, tiled=True)  30.2 us
    all_gather x1, blocking collectives, shards(): lax.all_gather(adapter_up_output, 'req', axis=0, tiled=True)  30.1 us
  transfers between devices with their start and end apart: 6, of which 3 were waited for; matrix products, arithmetic and copies ran while one was open for 8% of the time, Pallas kernels for 0%

commit v1 on v0

--- a/solution.py
+++ b/solution.py
@@ -80,7 +80,13 @@
 ):
     feature_group_count = lax.axis_size("mlp")
     feature_group_index = lax.axis_index("mlp")
-    whole = lax.all_gather(hidden_input, "mlp", axis=1, tiled=True)
+    devices = lax.axis_size("mlp")
+    held, parts = (hidden_input, [hidden_input])
+    for _ in range(devices - 1):
+        held = lax.ppermute(held, "mlp", [(i, (i + 1) % devices) for i in range(devices)])
+        parts.insert(0, held)
+    line = jnp.concatenate(parts, axis=1)
+    whole = jnp.roll(line, (lax.axis_index("mlp") + 1) * hidden_input.shape[1], axis=1)
     row_count, full_width = whole.shape
     normalized_input = root_mean_scale(whole.astype(jnp.float32), input_norm_gain).astype(
         jnp.bfloat16

time: 520 us -> 466 us (0.90)
  waiting for transfers between devices: 180 us -> 104 us
  starting transfers between devices: 0.23 us -> 30.3 us
  blocking collectives: 272 us -> 264 us
    ppermute x0 -> x15, waiting for transfers between devices: none -> 103 us  [shards(): lax.ppermute(held, 'mlp', [(i, (i + 1) % devices) for i in range(devices)])]
    all_gather x1 -> x0, waiting for transfers between devices: 63.1 us -> none  [shards(): whole = lax.all_gather(hidden_input, 'mlp', axis=1, tiled=True)]
    all_gather x1, waiting for transfers between devices: 61.2 us -> 0.01 us  [shards(): kv_part = lax.all_gather(own_wkv, 'req', axis=0, tiled=True)]
    all_gather x1, waiting for transfers between devices: 53.5 us -> 0.02 us  [shards(): lax.all_gather(output_weight, 'req', axis=2, tiled=True)]
    ppermute x0 -> x15, starting transfers between devices: none -> 30.1 us  [shards(): lax.ppermute(held, 'mlp', [(i, (i + 1) % devices) for i in range(devices)])]
  transfers between devices with their start and end apart: 6 -> 20, of which waited for: 3 -> 13; matrix products, arithmetic and copies ran while one was open for 8% -> 10% of each run, Pallas kernels for 0% -> 0%
where the time goes in v1:
time: 466 us; the launch traced here: 465 us
  blocking collectives  264 us (57%)
  waiting for transfers between devices  104 us (22%)
  starting transfers between devices  30.3 us (7%)
  matrix products  18.8 us (4%)
  other arithmetic  17.2 us (4%)
  local copies, waits for them, and re-layouts  15.8 us (3%)
  between operations  14.6 us (3%)
    ppermute x15, waiting for transfers between devices, shards(): lax.ppermute(held, 'mlp', [(i, (i + 1) % devices) for i in range(devices)])  103 us
    psum x1, blocking collectives, shards(): lax.psum(select_rows(low_terms, group_members).astype(jnp.bfloat16), 'mlp')  69.8 us
    psum x1, blocking collectives, shards(): lax.psum(select_rows(out_terms, group_members), 'mlp').astype(jnp.bfloat16)  69.6 us
    all_gather x1, blocking collectives, shards(): lax.all_gather(request_key_value_up, 'req', axis=0, tiled=True)  35.6 us
    all_gather x1, blocking collectives, shards(): lax.all_gather(adapter_up_query, 'req', axis=0, tiled=True)  30.6 us
    ppermute x15, starting transfers between devices, shards(): lax.ppermute(held, 'mlp', [(i, (i + 1) % devices) for i in range(devices)])  30.1 us
    all_gather x1, blocking collectives, shards(): lax.all_gather(adapter_up_output, 'req', axis=0, tiled=True)  29.6 us
    all_gather x1, blocking collectives, shards(): lax.all_gather(adapter_down_output, 'req', axis=0, tiled=True)  28.7 us
  transfers between devices with their start and end apart: 20, of which 13 were waited for; matrix products, arithmetic and copies ran while one was open for 10% of the time, Pallas kernels for 0%

profile of v1, /device:TPU:32, one launch (start us, length us, event | category | flops | bytes accessed | tf_op | source)
XLA Modules:
  0.0 465.1 jit_solution(3498082894791414444)
XLA Ops:
  9.7 3.4 collective-permute-start
  18.8 3.2 collective-permute-done
  21.9 1.9 collective-permute-start.1
  26.4 6.7 %collective-permute-done.1 = bf16[384,256]{1,0:T(8,128)(2,1)S(1)} collective-permute-done((bf16[384,256]{1,0:T(8,128)(2,1)S(1)}, bf16[384,256]{1,0:T(8,128)(2,1)S(1)}, u32[]{:S(2)}, u32[]{:S(2)}) %collective-permute-start.1) | collective-permute-done | bytes 196640 | tf_op jit(solution)/shard_map/ppermute | solution.py:86
  33.1 1.9 collective-permute-start.2
  35.6 8.3 %collective-permute-done.2 = bf16[384,256]{1,0:T(8,128)(2,1)S(1)} collective-permute-done((bf16[384,256]{1,0:T(8,128)(2,1)S(1)}, bf16[384,256]{1,0:T(8,128)(2,1)S(1)}, u32[]{:S(2)}, u32[]{:S(2)}) %collective-permute-start.2) | collective-permute-done | bytes 196640 | tf_op jit(solution)/shard_map/ppermute | solution.py:86
  48.2 6.6 %collective-permute-done.3 = bf16[384,256]{1,0:T(8,128)(2,1)S(1)} collective-permute-done((bf16[384,256]{1,0:T(8,128)(2,1)S(1)}, bf16[384,256]{1,0:T(8,128)(2,1)S(1)}, u32[]{:S(2)}, u32[]{:S(2)}) %collective-permute-start.3) | collective-permute-done | bytes 196640 | tf_op jit(solution)/shard_map/ppermute | solution.py:86
  54.8 1.9 collective-permute-start.4
  56.7 35.6 %all_gather.26 = bf16[64,16,2,128]{3,1,2,0:T(8,128)(2,1)S(1)} all-gather(bf16[2,16,2,128]{3,1,2,0:T(8,128)(2,1)S(1)} %copy.66), channel_id=1, replica_groups=mesh['req'=32,'mlp'=16] {'req'}, dimensions={0}, use_global_device_ids=true | all-gather | bytes 540672 | tf_op jit(solution)/shard_map/all_gather | solution.py:112
  92.9 1.9 collective-permute-start.5
  94.9 30.6 %all_gather.28 = bf16[64,16,256]{2,1,0:T(8,128)(2,1)S(1)} all-gather(bf16[2,16,256]{2,1,0:T(8,128)(2,1)} %param.29), channel_id=1, replica_groups=mesh['req'=32,'mlp'=16] {'req'}, dimensions={0}, use_global_device_ids=true | all-gather | bytes 540672 | tf_op jit(solution)/shard_map/all_gather | solution.py:111
  125.5 1.9 collective-permute-start.6
  128.1 10.1 %collective-permute-done.6 = bf16[384,256]{1,0:T(8,128)(2,1)S(1)} collective-permute-done((bf16[384,256]{1,0:T(8,128)(2,1)S(1)}, bf16[384,256]{1,0:T(8,128)(2,1)S(1)}, u32[]{:S(2)}, u32[]{:S(2)}) %collective-permute-start.6) | collective-permute-done | bytes 196640 | tf_op jit(solution)/shard_map/ppermute | solution.py:86
  138.1 1.9 collective-permute-start.7
  140.8 9.1 %collective-permute-done.7 = bf16[384,256]{1,0:T(8,128)(2,1)S(1)} collective-permute-done((bf16[384,256]{1,0:T(8,128)(2,1)S(1)}, bf16[384,256]{1,0:T(8,128)(2,1)S(1)}, u32[]{:S(2)}, u32[]{:S(2)}) %collective-permute-start.7) | collective-permute-done | bytes 196640 | tf_op jit(solution)/shard_map/ppermute | solution.py:86
  153.8 7.0 %collective-permute-done.8 = bf16[384,256]{1,0:T(8,128)(2,1)S(1)} collective-permute-done((bf16[384,256]{1,0:T(8,128)(2,1)S(1)}, bf16[384,256]{1,0:T(8,128)(2,1)S(1)}, u32[]{:S(2)}, u32[]{:S(2)}) %collective-permute-start.8) | collective-permute-done | bytes 196640 | tf_op jit(solution)/shard_map/ppermute | solution.py:86
  162.9 8.8 %collective-permute-done.9 = bf16[384,256]{1,0:T(8,128)(2,1)S(1)} collective-permute-done((bf16[384,256]{1,0:T(8,128)(2,1)S(1)}, bf16[384,256]{1,0:T(8,128)(2,1)S(1)}, u32[]{:S(2)}, u32[]{:S(2)}) %collective-permute-start.9) | collective-permute-done | bytes 196640 | tf_op jit(solution)/shard_map/ppermute | solution.py:86
  173.8 8.8 %collective-permute-done.10 = bf16[384,256]{1,0:T(8,128)(2,1)S(1)} collective-permute-done((bf16[384,256]{1,0:T(8,128)(2,1)S(1)}, bf16[384,256]{1,0:T(8,128)(2,1)S(1)}, u32[]{:S(2)}, u32[]{:S(2)}) %collective-permute-start.10) | collective-permute-done | bytes 196640 | tf_op jit(solution)/shard_map/ppermute | solution.py:86
  185.4 8.1 %collective-permute-done.11 = bf16[384,256]{1,0:T(8,128)(2,1)S(1)} collective-permute-done((bf16[384,256]{1,0:T(8,128)(2,1)S(1)}, bf16[384,256]{1,0:T(8,128)(2,1)S(1)}, u32[]{:S(2)}, u32[]{:S(2)}) %collective-permute-start.11) | collective-permute-done | bytes 196640 | tf_op jit(solution)/shard_map/ppermute | solution.py:86
  196.1 8.2 %collective-permute-done.12 = bf16[384,256]{1,0:T(8,128)(2,1)S(1)} collective-permute-done((bf16[384,256]{1,0:T(8,128)(2,1)S(1)}, bf16[384,256]{1,0:T(8,128)(2,1)S(1)}, u32[]{:S(2)}, u32[]{:S(2)}) %collective-permute-start.12) | collective-permute-done | bytes 196640 | tf_op jit(solution)/shard_map/ppermute | solution.py:86
  206.3 9.0 %collective-permute-done.13 = bf16[384,256]{1,0:T(8,128)(2,1)S(1)} collective-permute-done((bf16[384,256]{1,0:T(8,128)(2,1)S(1)}, bf16[384,256]{1,0:T(8,128)(2,1)S(1)}, u32[]{:S(2)}, u32[]{:S(2)}) %collective-permute-start.13) | collective-permute-done | bytes 196640 | tf_op jit(solution)/shard_map/ppermute | solution.py:86
  217.3 8.9 %collective-permute-done.14 = bf16[384,256]{1,0:T(8,128)(2,1)S(1)} collective-permute-done((bf16[384,256]{1,0:T(8,128)(2,1)S(1)}, bf16[384,256]{1,0:T(8,128)(2,1)S(1)}, u32[]{:S(2)}, u32[]{:S(2)}) %collective-permute-start.14) | collective-permute-done | bytes 196640 | tf_op jit(solution)/shard_map/ppermute | solution.py:86
  227.8 2.7 fusion.2
  230.5 2.0 gather_fusion.1
  233.6 69.8 %psum.14 = bf16[384,48]{0,1:T(8,128)(2,1)S(1)} all-reduce(bf16[384,48]{0,1:T(8,128)(2,1)S(1)} %fusion.25), channel_id=1, replica_groups=mesh['req'=32,'mlp'=16] {'mlp'}, use_global_device_ids=true, to_apply=%region_4.5 | all-reduce | flops 18432 | bytes 73728 | tf_op jit(solution)/shard_map/psum | solution.py:128
  305.6 4.7 %copy.61 = bf16[4096,2,128]{0,2,1:T(8,128)(2,1)S(1)} copy(bf16[4096,2,128]{2,1,0:T(2,128)(2,1)} %all-gather.5.cloned.1.call-done) | data formatting | bytes 4194304 | tf_op jit(solution)/shard_map/reshape | solution.py:134
  310.3 3.3 fusion.17
  315.9 3.9 multiply_reduce_fusion
  322.3 4.3 convolution_convert_fusion
  326.6 28.7 %all_gather.30 = bf16[64,16,256]{2,1,0:T(8,128)(2,1)S(1)} all-gather(bf16[2,16,256]{2,1,0:T(8,128)(2,1)S(1)} %copy-done.5), channel_id=1, replica_groups=mesh['req'=32,'mlp'=16] {'req'}, dimensions={0}, use_global_device_ids=true | all-gather | bytes 540672 | tf_op jit(solution)/shard_map/all_gather | solution.py:110
  355.9 29.6 %all_gather.31 = bf16[64,16,256]{2,1,0:T(8,128)(2,1)S(1)} all-gather(bf16[2,16,256]{2,1,0:T(8,128)(2,1)S(1)} %copy-done.6), channel_id=1, replica_groups=mesh['req'=32,'mlp'=16] {'req'}, dimensions={0}, use_global_device_ids=true | all-gather | bytes 540672 | tf_op jit(solution)/shard_map/all_gather | solution.py:113
  386.3 69.6 %psum.15 = bf16[384,16]{0,1:T(8,128)(2,1)S(1)} all-reduce(f32[384,16]{0,1:T(8,128)S(1)} %fusion.26), channel_id=1, replica_groups=mesh['req'=32,'mlp'=16] {'mlp'}, use_global_device_ids=true, to_apply=%region_12.14 | all-reduce | flops 6144 | bytes 36864 | tf_op jit(solution)/shard_map/psum | solution.py:204
  (139 shorter events, 48.0 us)
Async XLA Ops:
  7.2 1.0 copy-start
  7.2 219.4 %copy-start.1 = (bf16[384,256]{1,0:T(8,128)(2,1)S(1)}, bf16[384,256]{1,0:T(8,128)(2,1)}, u32[]{:S(2)}) copy-start(bf16[384,256]{1,0:T(8,128)(2,1)} %param.20) | copy-start | bytes 589828
  7.2 223.3 %all-gather.7.cloned.1.call-start = ((), (), s32[]{:S(2)}) async-start(), calls=%async_computation.2 | async-start | bytes 1622016 | tf_op jit(solution)/shard_map/all_gather | solution.py:109
  7.9 297.7 %all-gather.5.cloned.1.call-start = ((), (), s32[]{:S(2)}) async-start(), calls=%async_computation.1 | async-start | bytes 2162688 | tf_op jit(solution)/shard_map/all_gather | solution.py:130
  8.9 306.9 %all-gather.9.cloned.1.call-start = ((), (), s32[]{:S(2)}) async-start(), calls=%async_computation.3 | async-start | bytes 2162688 | tf_op jit(solution)/shard_map/all_gather | solution.py:129
  9.6 312.6 %all-gather.11.cloned.1.call-start = ((), (), s32[]{:S(2)}) async-start(), calls=%async_computation.4 | async-start | bytes 2162688 | tf_op jit(solution)/shard_map/all_gather | solution.py:208
  9.7 12.2 %collective-permute-start = (bf16[384,256]{1,0:T(8,128)(2,1)}, bf16[384,256]{1,0:T(8,128)(2,1)S(1)}, u32[]{:S(2)}, u32[]{:S(2)}) collective-permute-start(bf16[384,256]{1,0:T(8,128)(2,1)} %param.20), channel_id=1, source_target_pairs={{0,1},{1,2},{2,3},{3,4},{4,5},{5,6},{6,7},{7,8},{8,9},{9,10},{10,1... | collective-permute-start | bytes 589832 | tf_op jit(solution)/shard_map/ppermute | solution.py:86
  13.1 443.5 %reduce-scatter.2.cloned.1.call-start = ((), (), s32[]{:S(2)}) async-start(), calls=%async_computation.5 | async-start | bytes 3342336 | tf_op jit(solution)/shard_map/reduce_scatter | solution.py:211
  21.9 11.1 %collective-permute-start.1 = (bf16[384,256]{1,0:T(8,128)(2,1)S(1)}, bf16[384,256]{1,0:T(8,128)(2,1)S(1)}, u32[]{:S(2)}, u32[]{:S(2)}) collective-permute-start(bf16[384,256]{1,0:T(8,128)(2,1)S(1)} %collective-permute-done), channel_id=1, source_target_pairs={{0,1},{1,2},{2,3},{3,4},{4,5},{5,6},{6,7},{7,8},{8,9},{9,10},{10,1... | collective-permute-start | bytes 589832 | tf_op jit(solution)/shard_map/ppermute | solution.py:86
  33.1 10.9 %collective-permute-start.2 = (bf16[384,256]{1,0:T(8,128)(2,1)S(1)}, bf16[384,256]{1,0:T(8,128)(2,1)S(1)}, u32[]{:S(2)}, u32[]{:S(2)}) collective-permute-start(bf16[384,256]{1,0:T(8,128)(2,1)S(1)} %collective-permute-done.1), channel_id=1, source_target_pairs={{0,1},{1,2},{2,3},{3,4},{4,5},{5,6},{6,7},{7,8},{8,9},{9,10},{10,1... | collective-permute-start | bytes 589832 | tf_op jit(solution)/shard_map/ppermute | solution.py:86
  43.9 10.9 %collective-permute-start.3 = (bf16[384,256]{1,0:T(8,128)(2,1)S(1)}, bf16[384,256]{1,0:T(8,128)(2,1)S(1)}, u32[]{:S(2)}, u32[]{:S(2)}) collective-permute-start(bf16[384,256]{1,0:T(8,128)(2,1)S(1)} %collective-permute-done.2), channel_id=1, source_target_pairs={{0,1},{1,2},{2,3},{3,4},{4,5},{5,6},{6,7},{7,8},{8,9},{9,10},{10,1... | collective-permute-start | bytes 589832 | tf_op jit(solution)/shard_map/ppermute | solution.py:86
  54.8 38.1 %collective-permute-start.4 = (bf16[384,256]{1,0:T(8,128)(2,1)S(1)}, bf16[384,256]{1,0:T(8,128)(2,1)S(1)}, u32[]{:S(2)}, u32[]{:S(2)}) collective-permute-start(bf16[384,256]{1,0:T(8,128)(2,1)S(1)} %collective-permute-done.3), channel_id=1, source_target_pairs={{0,1},{1,2},{2,3},{3,4},{4,5},{5,6},{6,7},{7,8},{8,9},{9,10},{10,1... | collective-permute-start | bytes 589832 | tf_op jit(solution)/shard_map/ppermute | solution.py:86
  92.9 32.6 %collective-permute-start.5 = (bf16[384,256]{1,0:T(8,128)(2,1)S(1)}, bf16[384,256]{1,0:T(8,128)(2,1)S(1)}, u32[]{:S(2)}, u32[]{:S(2)}) collective-permute-start(bf16[384,256]{1,0:T(8,128)(2,1)S(1)} %collective-permute-done.4), channel_id=1, source_target_pairs={{0,1},{1,2},{2,3},{3,4},{4,5},{5,6},{6,7},{7,8},{8,9},{9,10},{10,1... | collective-permute-start | bytes 589832 | tf_op jit(solution)/shard_map/ppermute | solution.py:86
  125.5 12.6 %collective-permute-start.6 = (bf16[384,256]{1,0:T(8,128)(2,1)S(1)}, bf16[384,256]{1,0:T(8,128)(2,1)S(1)}, u32[]{:S(2)}, u32[]{:S(2)}) collective-permute-start(bf16[384,256]{1,0:T(8,128)(2,1)S(1)} %collective-permute-done.5), channel_id=1, source_target_pairs={{0,1},{1,2},{2,3},{3,4},{4,5},{5,6},{6,7},{7,8},{8,9},{9,10},{10,1... | collective-permute-start | bytes 589832 | tf_op jit(solution)/shard_map/ppermute | solution.py:86
  138.1 11.8 %collective-permute-start.7 = (bf16[384,256]{1,0:T(8,128)(2,1)S(1)}, bf16[384,256]{1,0:T(8,128)(2,1)S(1)}, u32[]{:S(2)}, u32[]{:S(2)}) collective-permute-start(bf16[384,256]{1,0:T(8,128)(2,1)S(1)} %collective-permute-done.6), channel_id=1, source_target_pairs={{0,1},{1,2},{2,3},{3,4},{4,5},{5,6},{6,7},{7,8},{8,9},{9,10},{10,1... | collective-permute-start | bytes 589832 | tf_op jit(solution)/shard_map/ppermute | solution.py:86
  149.9 10.9 %collective-permute-start.8 = (bf16[384,256]{1,0:T(8,128)(2,1)S(1)}, bf16[384,256]{1,0:T(8,128)(2,1)S(1)}, u32[]{:S(2)}, u32[]{:S(2)}) collective-permute-start(bf16[384,256]{1,0:T(8,128)(2,1)S(1)} %collective-permute-done.7), channel_id=1, source_target_pairs={{0,1},{1,2},{2,3},{3,4},{4,5},{5,6},{6,7},{7,8},{8,9},{9,10},{10,1... | collective-permute-start | bytes 589832 | tf_op jit(solution)/shard_map/ppermute | solution.py:86
  160.8 10.9 %collective-permute-start.9 = (bf16[384,256]{1,0:T(8,128)(2,1)S(1)}, bf16[384,256]{1,0:T(8,128)(2,1)S(1)}, u32[]{:S(2)}, u32[]{:S(2)}) collective-permute-start(bf16[384,256]{1,0:T(8,128)(2,1)S(1)} %collective-permute-done.8), channel_id=1, source_target_pairs={{0,1},{1,2},{2,3},{3,4},{4,5},{5,6},{6,7},{7,8},{8,9},{9,10},{10,1... | collective-permute-start | bytes 589832 | tf_op jit(solution)/shard_map/ppermute | solution.py:86
  171.7 10.9 %collective-permute-start.10 = (bf16[384,256]{1,0:T(8,128)(2,1)S(1)}, bf16[384,256]{1,0:T(8,128)(2,1)S(1)}, u32[]{:S(2)}, u32[]{:S(2)}) collective-permute-start(bf16[384,256]{1,0:T(8,128)(2,1)S(1)} %collective-permute-done.9), channel_id=1, source_target_pairs={{0,1},{1,2},{2,3},{3,4},{4,5},{5,6},{6,7},{7,8},{8,9},{9,10},{10,1... | collective-permute-start | bytes 589832 | tf_op jit(solution)/shard_map/ppermute | solution.py:86
  182.5 10.9 %collective-permute-start.11 = (bf16[384,256]{1,0:T(8,128)(2,1)S(1)}, bf16[384,256]{1,0:T(8,128)(2,1)S(1)}, u32[]{:S(2)}, u32[]{:S(2)}) collective-permute-start(bf16[384,256]{1,0:T(8,128)(2,1)S(1)} %collective-permute-done.10), channel_id=1, source_target_pairs={{0,1},{1,2},{2,3},{3,4},{4,5},{5,6},{6,7},{7,8},{8,9},{9,10},{10,1... | collective-permute-start | bytes 589832 | tf_op jit(solution)/shard_map/ppermute | solution.py:86
  184.5 42.5 %copy-start.9 = (f32[64]{0:T(128)}, f32[64]{0:T(128)S(1)}, u32[]{:S(2)}) copy-start(f32[64]{0:T(128)S(1)} %multiply_exponential_fusion) | copy-start | bytes 772
  193.4 10.9 %collective-permute-start.12 = (bf16[384,256]{1,0:T(8,128)(2,1)S(1)}, bf16[384,256]{1,0:T(8,128)(2,1)S(1)}, u32[]{:S(2)}, u32[]{:S(2)}) collective-permute-start(bf16[384,256]{1,0:T(8,128)(2,1)S(1)} %collective-permute-done.11), channel_id=1, source_target_pairs={{0,1},{1,2},{2,3},{3,4},{4,5},{5,6},{6,7},{7,8},{8,9},{9,10},{10,1... | collective-permute-start | bytes 589832 | tf_op jit(solution)/shard_map/ppermute | solution.py:86
  204.3 11.0 %collective-permute-start.13 = (bf16[384,256]{1,0:T(8,128)(2,1)S(1)}, bf16[384,256]{1,0:T(8,128)(2,1)S(1)}, u32[]{:S(2)}, u32[]{:S(2)}) collective-permute-start(bf16[384,256]{1,0:T(8,128)(2,1)S(1)} %collective-permute-done.12), channel_id=1, source_target_pairs={{0,1},{1,2},{2,3},{3,4},{4,5},{5,6},{6,7},{7,8},{8,9},{9,10},{10,1... | collective-permute-start | bytes 589832 | tf_op jit(solution)/shard_map/ppermute | solution.py:86
  215.3 10.9 %collective-permute-start.14 = (bf16[384,256]{1,0:T(8,128)(2,1)S(1)}, bf16[384,256]{1,0:T(8,128)(2,1)S(1)}, u32[]{:S(2)}, u32[]{:S(2)}) collective-permute-start(bf16[384,256]{1,0:T(8,128)(2,1)S(1)} %collective-permute-done.13), channel_id=1, source_target_pairs={{0,1},{1,2},{2,3},{3,4},{4,5},{5,6},{6,7},{7,8},{8,9},{9,10},{10,1... | collective-permute-start | bytes 589832 | tf_op jit(solution)/shard_map/ppermute | solution.py:86
  217.3 15.2 %copy-start.7 = (f32[384,4]{0,1:T(4,128)}, f32[384,4]{0,1:T(4,128)S(1)}, u32[]{:S(2)}) copy-start(f32[384,4]{0,1:T(4,128)S(1)} %get-tuple-element.17) | copy-start | bytes 18436
  226.9 76.5 %copy-start.4 = (bf16[4,16,256]{2,1,0:T(8,128)(2,1)S(1)}, bf16[4,16,256]{2,1,0:T(8,128)(2,1)}, u32[]{:S(2)}) copy-start(bf16[4,16,256]{2,1,0:T(8,128)(2,1)} %gather_fusion.3) | copy-start | bytes 98308
  313.6 6.4 %copy-start.10 = (f32[128]{0:T(128)S(1)}, f32[128]{0:T(128)}, u32[]{:S(2)}) copy-start(f32[128]{0:T(128)} %convert_element_type.112) | copy-start | bytes 1540
  313.6 6.8 %copy-start.2 = (pred[384,896]{0,1:T(8,128)(4,1)S(1)}, pred[384,896]{0,1:T(8,128)(4,1)}, u32[]{:S(2)}) copy-start(pred[384,896]{0,1:T(8,128)(4,1)} %pad_add_fusion) | copy-start | bytes 1032196
  313.6 6.8 %copy-start.3 = (bf16[512,1,128]{2,0,1:T(8,128)(2,1)S(1)}, bf16[512,1,128]{2,0,1:T(8,128)(2,1)}, u32[]{:S(2)}) copy-start(bf16[512,1,128]{2,0,1:T(8,128)(2,1)} %copy.67) | copy-start | bytes 393220
  322.2 4.4 copy-start.5
  322.2 33.6 %copy-start.6 = (bf16[2,16,256]{2,1,0:T(8,128)(2,1)S(1)}, bf16[2,16,256]{2,1,0:T(8,128)(2,1)}, u32[]{:S(2)}) copy-start(bf16[2,16,256]{2,1,0:T(8,128)(2,1)} %param.31) | copy-start | bytes 49156
  322.3 63.8 %copy-start.8 = (f32[384,4]{0,1:T(4,128)S(1)}, f32[384,4]{0,1:T(4,128)}, u32[]{:S(2)}) copy-start(f32[384,4]{0,1:T(4,128)} %copy-done.7) | copy-start | bytes 18436
Sparse Core Ops, SparseCore 0:
  10.1 75.3 all-gather.6
  88.3 68.7 all-gather.4
  159.2 68.8 all-gather.8
  230.0 70.6 all-gather.10
  326.7 83.1 reduce-scatter.1
